TPU v7x, 128 devices: a whole 4x4x4 slice. The times are simulated.
128 devices in a mesh: ao: 32 (over x, y, z_hi), aux: 4 (over z_lo, core).
Axes of the slice: x: 4, y: 4, z: 4 (z_hi: 2, z_lo: 2; z = z_hi * 2 + z_lo), core: 2. Of those that a mesh axis runs over, the one named last changes fastest.
Arguments:
- tensor: bfloat16 [64, 4096, 384], P('aux', 'ao'), may hold values from -0.15625 to 0.15625
- pattern: int32 [64, 96], P('aux', 'ao'), may hold values 0 or 1
- occ_density: bfloat16 [4096, 384], P('ao'), may hold values from -0.3125 to 0.3125
- virt_density: bfloat16 [4096, 384], P('ao'), may hold values from -0.3125 to 0.3125
Outputs:
- polarizability: float32 [64, 64], P('aux')
All inputs are finite; a program needn't handle non-finite values. No bound on the sum of `pattern` on one device may be relied on, other than what follows from the above.
Results may differ from a plain program's by a relative error of at most 0.0041.
Values may be sent and summed in bfloat16 or wider, within the bound.
A program may use at most 128 MiB of HBM per device.

v0:
```python
import jax
import jax.numpy as jnp
from jax import lax
from jax.sharding import PartitionSpec as P

AB = 128


def extended(cells, sides, width):
    for axis, dim in sides:
        count = lax.axis_size(axis)
        head = lax.slice_in_dim(cells, 0, width, axis=dim)
        tail = lax.slice_in_dim(cells, cells.shape[dim] - width, cells.shape[dim], axis=dim)
        cells = jnp.concatenate(
            [
                lax.ppermute(tail, axis, [(i, (i + 1) % count) for i in range(count)]),
                cells,
                lax.ppermute(head, axis, [((i + 1) % count, i) for i in range(count)]),
            ],
            axis=dim,
        )
    return cells


def copy_for_each(shard, axis):
    size = lax.axis_size(axis)
    return lax.all_to_all(
        jnp.broadcast_to(shard[None], (size, *shard.shape)), axis, 0, 0, tiled=True
    )


def taken_together(shard, axis):
    everything = copy_for_each(shard, axis)
    return jnp.sum(everything, axis=0)


def occ_side(masked, occ_rims, blocks):
    aux_count = masked.shape[0]
    factor_rows = masked.reshape(aux_count, blocks, AB, 3, AB)
    partner = occ_rims.reshape(blocks + 2, AB, 3, AB)
    pieces = [None] * 5
    for offset_a in range(3):
        for offset_b in range(3):
            term = jnp.einsum(
                "qlik,lkj->qlij",
                factor_rows[:, :, :, offset_a, :],
                partner[offset_a : offset_a + blocks, :, offset_b, :],
                preferred_element_type=jnp.float32,
            )
            slot = offset_a + offset_b
            pieces[slot] = term if pieces[slot] is None else pieces[slot] + term
    return jnp.stack(pieces, axis=3).astype(jnp.bfloat16).reshape(aux_count, -1)


def virt_side(virt_density, tensor_rims, blocks):
    aux_count = tensor_rims.shape[0]
    factor_rows = virt_density.reshape(blocks, AB, 3, AB)
    partner = tensor_rims.reshape(aux_count, blocks + 2, AB, 3, AB)
    pieces = [None] * 5
    for offset_a in range(3):
        for offset_b in range(3):
            term = jnp.einsum(
                "lik,qlkj->qlij",
                factor_rows[:, :, offset_a, :],
                partner[:, offset_a : offset_a + blocks, :, offset_b, :],
                preferred_element_type=jnp.float32,
            )
            slot = offset_a + offset_b
            pieces[slot] = term if pieces[slot] is None else pieces[slot] + term
    return jnp.stack(pieces, axis=3).astype(jnp.bfloat16).reshape(aux_count, -1)


def on_device(tensor, pattern, occ_density, virt_density):
    aux_count = tensor.shape[0]
    blocks = tensor.shape[1] // AB
    masked = (
        tensor.reshape(aux_count, blocks, AB, 3, AB)
        * pattern.reshape(aux_count, blocks, 1, 3, 1).astype(jnp.bfloat16)
    ).reshape(tensor.shape)
    occ_rims = extended(occ_density, (("ao", 0),), AB)
    occ_flat = occ_side(masked, occ_rims, blocks)
    own_rims = extended(masked, (("ao", 1),), AB)
    virt_flat = virt_side(virt_density, own_rims, blocks)
    columns = jnp.einsum(
        "pl,ql->pq",
        occ_flat,
        lax.all_gather(virt_flat, "aux", axis=0, tiled=True),
        preferred_element_type=jnp.float32,
    )
    return taken_together(columns, "ao")


def solution(mesh):
    return jax.shard_map(
        on_device,
        mesh=mesh,
        in_specs=(P("aux", "ao", None), P("aux", "ao"), P("ao", None), P("ao", None)),
        out_specs=P("aux", None),
        check_vma=False,
    )
```

profile of v0, /device:TPU:1, one launch (start us, length us, event | category | flops | bytes accessed | tf_op | source)
XLA Modules:
  0.0 298.7 jit_solution(1570233315929819093)
XLA Ops:
  7.5 1.6 broadcast_multiply_fusion
  9.0 9.1 %collective-permute-start.3 = (bf16[16,128,384]{2,1,0:T(8,128)(2,1)S(1)}, bf16[16,128,384]{2,1,0:T(8,128)(2,1)S(1)}, u32[]{:S(2)}, u32[]{:S(2)}) collective-permute-start(bf16[16,128,384]{2,1,0:T(8,128)(2,1)S(1)} %broadcast_multiply_fusion), channel_id=1, source_target_pairs={{4,0},{8,4},{12,8},{16,12},{20,16},{24,20},{28,24},{32,28},{36,32}... | collective-permute-start | bytes 4718600 | tf_op jit(solution)/shard_map/ppermute | solution.py:18
  18.3 63.0 %collective-permute-done.3 = bf16[16,128,384]{2,1,0:T(8,128)(2,1)S(1)} collective-permute-done((bf16[16,128,384]{2,1,0:T(8,128)(2,1)S(1)}, bf16[16,128,384]{2,1,0:T(8,128)(2,1)S(1)}, u32[]{:S(2)}, u32[]{:S(2)}) %collective-permute-start.3) | collective-permute-done | bytes 1572896 | tf_op jit(solution)/shard_map/ppermute | solution.py:18
  82.2 3.6 %pad_maximum_fusion = bf16[16,384,384]{2,1,0:T(8,128)(2,1)} fusion(bf16[16,128,384]{2,1,0:T(8,128)(2,1)S(1)} %collective-permute-done.3, bf16[16,128,384]{2,1,0:T(8,128)(2,1)S(1)} %broadcast_multiply_fusion, bf16[16,128,384]{2,1,0:T(8,128)(2,1)} %collective-permute-done.2), kind=kLoop, calls=%fused_computation | loop fusion | flops 14155776 | bytes 9437184 | tf_op jit(solution)/shard_map/concatenate | solution.py:14
  85.9 12.9 %reshape.260 = bf16[16,3,128,3,128]{4,3,2,1,0:T(4,128)(2,1)} reshape(bf16[16,384,384]{2,1,0:T(8,128)(2,1)} %pad_maximum_fusion) | data formatting | bytes 9437184 | tf_op jit(solution)/shard_map/reshape | solution.py:58
  98.8 14.0 %fusion.50 = (bf16[16,1,128,1,128]{4,3,2,1,0:T(2,128)(2,1)S(1)}, bf16[16,1,128,1,128]{4,3,2,1,0:T(2,128)(2,1)S(1)}, bf16[16,1,128,1,128]{4,3,2,1,0:T(2,128)(2,1)...) fusion(bf16[16,3,128,3,128]{4,3,2,1,0:T(4,128)(2,1)} %reshape.260), kind=kLoop, calls=%fused_computation.73 | loop fusion | bytes 9437184 | tf_op jit(solution)/shard_map/slice | solution.py:65
  112.9 3.5 %copy.69 = bf16[16,1,128,1,128]{2,4,0,3,1:T(8,128)(2,1)} copy(bf16[16,1,128,1,128]{4,3,2,1,0:T(2,128)(2,1)} %get-tuple-element.13) | data formatting | bytes 1048576
  116.3 3.5 %copy.71 = bf16[16,1,128,1,128]{2,4,0,3,1:T(8,128)(2,1)} copy(bf16[16,1,128,1,128]{4,3,2,1,0:T(2,128)(2,1)} %get-tuple-element.12) | data formatting | bytes 1048576
  119.8 2.1 fusion.11
  121.9 2.3 fusion.35
  124.2 3.5 %copy.72 = bf16[16,1,128,1,128]{2,4,0,3,1:T(8,128)(2,1)} copy(bf16[16,1,128,1,128]{4,3,2,1,0:T(2,128)(2,1)} %get-tuple-element.11) | data formatting | bytes 1048576
  127.7 3.5 %copy.74 = bf16[16,1,128,1,128]{2,4,0,3,1:T(8,128)(2,1)} copy(bf16[16,1,128,1,128]{4,3,2,1,0:T(2,128)(2,1)} %get-tuple-element.10) | data formatting | bytes 1048576
  131.1 2.3 fusion.32
  133.4 3.5 %copy.75 = bf16[16,1,128,1,128]{2,4,0,3,1:T(8,128)(2,1)} copy(bf16[16,1,128,1,128]{4,3,2,1,0:T(2,128)(2,1)} %get-tuple-element.9) | data formatting | bytes 1048576
  136.9 3.5 %copy.76 = bf16[16,1,128,1,128]{2,4,0,3,1:T(8,128)(2,1)} copy(bf16[16,1,128,1,128]{4,3,2,1,0:T(2,128)(2,1)} %get-tuple-element.8) | data formatting | bytes 1048576
  140.4 1.8 copy.78
  142.2 2.3 fusion.28
  144.5 1.8 copy.79
  147.0 1.7 convolution_add_fusion.2
  153.1 6.1 %copy.59 = bf16[16,1,128,5,128]{4,3,2,0,1:T(8,128)(2,1)} copy(bf16[16,1,128,5,128]{2,4,0,3,1:T(8,128)(2,1)} %fusion.13) | data formatting | bytes 5242880 | tf_op jit(solution)/shard_map/stack | solution.py:70
  159.2 5.5 %convert_element_type.20 = bf16[16,81920]{1,0:T(8,128)(2,1)} reshape(bf16[16,1,128,5,128]{4,3,2,0,1:T(8,128)(2,1)} %copy.59) | data formatting | bytes 5242880 | tf_op jit(solution)/shard_map/convert_element_type | solution.py:70
  165.6 6.7 %collective-permute-start.1 = (bf16[128,384]{1,0:T(8,128)(2,1)S(1)}, bf16[128,384]{1,0:T(8,128)(2,1)S(1)}, u32[]{:S(2)}, u32[]{:S(2)}) collective-permute-start(bf16[128,384]{1,0:T(8,128)(2,1)S(1)} %copy-done.6), channel_id=1, source_target_pairs={{4,0},{8,4},{12,8},{16,12},{20,16},{24,20},{28,24},{32,28},{36,32}... | collective-permute-start | bytes 294920 | tf_op jit(solution)/shard_map/ppermute | solution.py:18
  172.3 1.6 copy.34
  173.9 1.9 copy.35
  176.0 5.5 %collective-permute-done = bf16[128,384]{1,0:T(8,128)(2,1)S(1)} collective-permute-done((bf16[128,384]{1,0:T(8,128)(2,1)S(1)}, bf16[128,384]{1,0:T(8,128)(2,1)S(1)}, u32[]{:S(2)}, u32[]{:S(2)}) %collective-permute-start) | collective-permute-done | bytes 98336 | tf_op jit(solution)/shard_map/ppermute | solution.py:16
  185.2 1.1 fusion.25
  188.8 1.1 fusion.9
  189.9 6.1 %copy.44 = bf16[16,1,128,5,128]{4,3,2,0,1:T(8,128)(2,1)} copy(bf16[16,1,128,5,128]{2,4,0,3,1:T(8,128)(2,1)} %fusion.9) | data formatting | bytes 5242880 | tf_op jit(solution)/shard_map/stack | solution.py:52
  196.1 4.5 %convert_element_type.19 = bf16[16,81920]{1,0:T(8,128)(2,1)S(1)} reshape(bf16[16,1,128,5,128]{4,3,2,0,1:T(8,128)(2,1)} %copy.44) | data formatting | bytes 5242880 | tf_op jit(solution)/shard_map/convert_element_type | solution.py:52
  200.5 65.5 %all-gather.2.cloned.1.call-done = bf16[64,81920]{1,0:T(8,128)(2,1)} async-done(((bf16[16,81920]{1,0:T(8,128)(2,1)}), bf16[64,81920]{1,0:T(8,128)(2,1)}) %all-gather.2.cloned.1.call-update) | async-done | bytes 10485776 | tf_op jit(solution)/shard_map/all_gather | solution.py:87
  266.0 5.5 %fusion.52 = f32[16,64]{1,0:T(8,128)S(1)} fusion(bf16[16,81920]{1,0:T(8,128)(2,1)S(1)} %convert_element_type.19, bf16[64,81920]{1,0:T(8,128)(2,1)} %all-gather.2.cloned.1.call-done), kind=kOutput, calls=%fused_computation.75 | convolution fusion | flops 167772160 | bytes 13111296 | tf_op jit(solution)/shard_map/pl,ql->pq/dot_general | solution.py:84
  271.7 17.9 %all_to_all.5 = f32[32,1,1024]{2,1,0:T(1,128)S(1)} all-to-all(f32[32,1,1024]{2,1,0:T(1,128)S(1)} %reshape.286), channel_id=1, replica_groups=mesh['ao'=32,'aux'=4] {'ao'}, dimensions={0} | all-to-all | bytes 262144 | tf_op jit(solution)/shard_map/all_to_all | solution.py:27
  (58 shorter events, 16.7 us)
Async XLA Ops:
  6.5 11.6 %copy-start.7 = (bf16[128,384]{1,0:T(8,128)(2,1)S(1)}, bf16[128,384]{1,0:T(8,128)(2,1)}, u32[]{:S(2)}) copy-start(bf16[128,384]{1,0:T(8,128)(2,1)} %param.7) | copy-start | bytes 294916
  6.5 259.5 %all-gather.2.cloned.1.call-start = ((), (), s32[]{:S(2)}) async-start(), calls=%async_computation.1 | async-start | bytes 13107200 | tf_op jit(solution)/shard_map/all_gather | solution.py:87
  9.0 72.3 %collective-permute-start.3 = (bf16[16,128,384]{2,1,0:T(8,128)(2,1)S(1)}, bf16[16,128,384]{2,1,0:T(8,128)(2,1)S(1)}, u32[]{:S(2)}, u32[]{:S(2)}) collective-permute-start(bf16[16,128,384]{2,1,0:T(8,128)(2,1)S(1)} %broadcast_multiply_fusion), channel_id=1, source_target_pairs={{4,0},{8,4},{12,8},{16,12},{20,16},{24,20},{28,24},{32,28},{36,32}... | collective-permute-start | bytes 4718600 | tf_op jit(solution)/shard_map/ppermute | solution.py:18
  18.2 64.1 %collective-permute-start.2 = (bf16[16,128,384]{2,1,0:T(8,128)(2,1)S(1)}, bf16[16,128,384]{2,1,0:T(8,128)(2,1)}, u32[]{:S(2)}, u32[]{:S(2)}) collective-permute-start(bf16[16,128,384]{2,1,0:T(8,128)(2,1)S(1)} %broadcast_multiply_fusion), channel_id=1, source_target_pairs={{0,4},{4,8},{8,12},{12,16},{16,20},{20,24},{24,28},{28,32},{32,36}... | collective-permute-start | bytes 4718600 | tf_op jit(solution)/shard_map/ppermute | solution.py:16
  144.5 4.2 %copy-start.1 = (f32[16,128,128]{2,1,0:T(8,128)S(1)}, f32[16,128,128]{2,1,0:T(8,128)}, u32[]{:S(2)}) copy-start(f32[16,128,128]{2,1,0:T(8,128)} %fusion.35) | copy-start | bytes 3145732
  146.3 2.5 copy-start.3
  147.0 2.9 copy-start.4
  148.8 2.2 copy-start.2
  148.8 2.2 copy-start.5
  164.7 0.9 copy-start.6
  164.7 7.6 %copy-start = (bf16[16,128,384]{2,1,0:T(8,128)(2,1)S(1)}, bf16[16,128,384]{2,1,0:T(8,128)(2,1)}, u32[]{:S(2)}) copy-start(bf16[16,128,384]{2,1,0:T(8,128)(2,1)} %param.4) | copy-start | bytes 4718596
  165.6 10.4 %collective-permute-start.1 = (bf16[128,384]{1,0:T(8,128)(2,1)S(1)}, bf16[128,384]{1,0:T(8,128)(2,1)S(1)}, u32[]{:S(2)}, u32[]{:S(2)}) collective-permute-start(bf16[128,384]{1,0:T(8,128)(2,1)S(1)} %copy-done.6), channel_id=1, source_target_pairs={{4,0},{8,4},{12,8},{16,12},{20,16},{24,20},{28,24},{32,28},{36,32}... | collective-permute-start | bytes 294920 | tf_op jit(solution)/shard_map/ppermute | solution.py:18
  172.3 9.2 %collective-permute-start = (bf16[128,384]{1,0:T(8,128)(2,1)S(1)}, bf16[128,384]{1,0:T(8,128)(2,1)S(1)}, u32[]{:S(2)}, u32[]{:S(2)}) collective-permute-start(bf16[128,384]{1,0:T(8,128)(2,1)S(1)} %copy-done.6), channel_id=1, source_target_pairs={{0,4},{4,8},{8,12},{12,16},{16,20},{20,24},{24,28},{28,32},{32,36}... | collective-permute-start | bytes 294920 | tf_op jit(solution)/shard_map/ppermute | solution.py:16
Sparse Core Ops, SparseCore 0:
  164.8 101.1 all-gather.1
where the time goes:
time: 300 us; the launch traced here: 299 us
  waiting for transfers between devices  135 us (45%)
  local copies, waits for them, and re-layouts  81.4 us (27%)
  matrix products  27.3 us (9%)
  blocking collectives  17.9 us (6%)
  starting transfers between devices  15.8 us (5%)
  between operations  13.6 us (5%)
  other arithmetic  7.71 us (3%)
    all_gather x1, waiting for transfers between devices, on_device(): lax.all_gather(virt_flat, 'aux', axis=0, tiled=True)  65.5 us
    ppermute x2, waiting for transfers between devices, extended(): lax.ppermute(head, axis, [((i + 1) % count, i) for i in range(count)])  63.1 us
    unnamed x39, local copies, waits for them, and re-layouts  29.1 us
    all_to_all x1, blocking collectives, copy_for_each(): lax.all_to_all(jnp.broadcast_to(shard[None], (size, *shard.shape)), axis,...  17.9 us
    ppermute x2, starting transfers between devices, extended(): lax.ppermute(head, axis, [((i + 1) % count, i) for i in range(count)])  15.8 us
    dot_general x9, matrix products, virt_side(): jnp.einsum('lik,qlkj->qlij', factor_rows[:, :, offset_a, :], partner[:, o...  15.1 us
    slice x1, local copies, waits for them, and re-layouts, virt_side(): partner[:, offset_a:offset_a + blocks, :, offset_b, :]  14 us
    reshape x1, local copies, waits for them, and re-layouts, virt_side(): partner = tensor_rims.reshape(aux_count, blocks + 2, AB, 3, AB)  12.9 us
  transfers between devices with their start and end apart: 5, of which 4 were waited for; matrix products, arithmetic and copies ran while one was open for 8% of the time, Pallas kernels for 0%

commit v1 on v0

--- a/solution.py
+++ b/solution.py
@@ -84,7 +84,9 @@
     columns = jnp.einsum(
         "pl,ql->pq",
         occ_flat,
-        lax.all_gather(virt_flat, "aux", axis=0, tiled=True),
+        jnp.concatenate(
+            lax.all_to_all(jnp.stack([virt_flat] * lax.axis_size("aux")), "aux", 0, 0), axis=0
+        ),
         preferred_element_type=jnp.float32,
     )
     return taken_together(columns, "ao")

time: 300 us -> 334 us (1.11)
  waiting for transfers between devices: 135 us -> 172 us
  between operations: 13.6 us -> 0.26 us
  starting transfers between devices: 15.8 us -> 24.4 us
    ppermute x2, waiting for transfers between devices: 6.36 us -> 168 us  [extended(): lax.ppermute(tail, axis, [(i, (i + 1) % count) for i in range(count)])]
    all_gather x1 -> x0, waiting for transfers between devices: 65.5 us -> none  [on_device(): lax.all_gather(virt_flat, 'aux', axis=0, tiled=True)]
    ppermute x2, waiting for transfers between devices: 63.1 us -> 4.07 us  [extended(): lax.ppermute(head, axis, [((i + 1) % count, i) for i in range(count)])]
    all_to_all x0 -> x1, starting transfers between devices: none -> 8 us  [on_device(): lax.all_to_all(jnp.stack([virt_flat] * lax.axis_size('aux')), 'aux', 0, 0)]
    another operation x0 -> x1, local copies, waits for them, and re-layouts: none -> 4.5 us  [on_device(): jnp.stack([virt_flat] * lax.axis_size('aux'))]
    ppermute x2, starting transfers between devices: 0.01 us -> 4.5 us  [extended(): lax.ppermute(tail, axis, [(i, (i + 1) % count) for i in range(count)])]
    ppermute x2, starting transfers between devices: 15.8 us -> 11.9 us  [extended(): lax.ppermute(head, axis, [((i + 1) % count, i) for i in range(count)])]
  transfers between devices with their start and end apart: 5 -> 5, of which waited for: 4 -> 4; matrix products, arithmetic and copies ran while one was open for 8% -> 7% of each run, Pallas kernels for 0% -> 0%
where the time goes in v1:
time: 334 us; the launch traced here: 332 us
  waiting for transfers between devices  172 us (51%)
  local copies, waits for them, and re-layouts  84.3 us (25%)
  matrix products  27.5 us (8%)
  starting transfers between devices  24.4 us (7%)
  blocking collectives  15.8 us (5%)
  other arithmetic  7.7 us (2%)
    ppermute x2, waiting for transfers between devices, extended(): lax.ppermute(tail, axis, [(i, (i + 1) % count) for i in range(count)])  168 us
    unnamed x39, local copies, waits for them, and re-layouts  28.4 us
    all_to_all x1, blocking collectives, copy_for_each(): lax.all_to_all(jnp.broadcast_to(shard[None], (size, *shard.shape)), axis,...  15.8 us
    dot_general x9, matrix products, virt_side(): jnp.einsum('lik,qlkj->qlij', factor_rows[:, :, offset_a, :], partner[:, o...  15.1 us
    slice x1, local copies, waits for them, and re-layouts, virt_side(): partner[:, offset_a:offset_a + blocks, :, offset_b, :]  14.1 us
    reshape x1, local copies, waits for them, and re-layouts, virt_side(): partner = tensor_rims.reshape(aux_count, blocks + 2, AB, 3, AB)  12.9 us
    ppermute x2, starting transfers between devices, extended(): lax.ppermute(head, axis, [((i + 1) % count, i) for i in range(count)])  11.9 us
    all_to_all x1, starting transfers between devices, on_device(): lax.all_to_all(jnp.stack([virt_flat] * lax.axis_size('aux')), 'aux', 0, 0)  8 us
  transfers between devices with their start and end apart: 5, of which 4 were waited for; matrix products, arithmetic and copies ran while one was open for 7% of the time, Pallas kernels for 0%

profile of v1, /device:TPU:1, one launch (start us, length us, event | category | flops | bytes accessed | tf_op | source)
XLA Modules:
  0.0 332.1 jit_solution(645961900090640807)
XLA Ops:
  2.5 4.5 %collective-permute-start.2 = (bf16[16,128,384]{2,1,0:T(8,128)(2,1)S(1)}, bf16[16,128,384]{2,1,0:T(8,128)(2,1)S(1)}, u32[]{:S(2)}, u32[]{:S(2)}) collective-permute-start(bf16[16,128,384]{2,1,0:T(8,128)(2,1)S(1)} %broadcast_multiply_fusion), channel_id=1, source_target_pairs={{0,4},{4,8},{8,12},{12,16},{16,20},{20,24},{24,28},{28,32},{32,36}... | collective-permute-start | bytes 4718600 | tf_op jit(solution)/shard_map/ppermute | solution.py:16
  7.0 4.7 %collective-permute-start.3 = (bf16[16,128,384]{2,1,0:T(8,128)(2,1)S(1)}, bf16[16,128,384]{2,1,0:T(8,128)(2,1)}, u32[]{:S(2)}, u32[]{:S(2)}) collective-permute-start(bf16[16,128,384]{2,1,0:T(8,128)(2,1)S(1)} %broadcast_multiply_fusion), channel_id=1, source_target_pairs={{4,0},{8,4},{12,8},{16,12},{20,16},{24,20},{28,24},{32,28},{36,32}... | collective-permute-start | bytes 4718600 | tf_op jit(solution)/shard_map/ppermute | solution.py:18
  11.8 61.9 %collective-permute-done.2 = bf16[16,128,384]{2,1,0:T(8,128)(2,1)S(1)} collective-permute-done((bf16[16,128,384]{2,1,0:T(8,128)(2,1)S(1)}, bf16[16,128,384]{2,1,0:T(8,128)(2,1)S(1)}, u32[]{:S(2)}, u32[]{:S(2)}) %collective-permute-start.2) | collective-permute-done | bytes 1572896 | tf_op jit(solution)/shard_map/ppermute | solution.py:16
  73.8 3.5 %collective-permute-done.3 = bf16[16,128,384]{2,1,0:T(8,128)(2,1)} collective-permute-done((bf16[16,128,384]{2,1,0:T(8,128)(2,1)S(1)}, bf16[16,128,384]{2,1,0:T(8,128)(2,1)}, u32[]{:S(2)}, u32[]{:S(2)}) %collective-permute-start.3) | collective-permute-done | bytes 1572896 | tf_op jit(solution)/shard_map/ppermute | solution.py:18
  77.2 3.6 %pad_maximum_fusion = bf16[16,384,384]{2,1,0:T(8,128)(2,1)} fusion(bf16[16,128,384]{2,1,0:T(8,128)(2,1)} %collective-permute-done.3, bf16[16,128,384]{2,1,0:T(8,128)(2,1)S(1)} %broadcast_multiply_fusion, bf16[16,128,384]{2,1,0:T(8,128)(2,1)S(1)} %collective-permute-done.2), kind=kLoop, calls=%fused_computation | loop fusion | flops 14155776 | bytes 9437184 | tf_op jit(solution)/shard_map/concatenate | solution.py:14
  80.9 12.9 %reshape.333 = bf16[16,3,128,3,128]{4,3,2,1,0:T(4,128)(2,1)} reshape(bf16[16,384,384]{2,1,0:T(8,128)(2,1)} %pad_maximum_fusion) | data formatting | bytes 9437184 | tf_op jit(solution)/shard_map/reshape | solution.py:58
  93.8 14.1 %fusion.50 = (bf16[16,1,128,1,128]{4,3,2,1,0:T(2,128)(2,1)S(1)}, bf16[16,1,128,1,128]{4,3,2,1,0:T(2,128)(2,1)S(1)}, bf16[16,1,128,1,128]{4,3,2,1,0:T(2,128)(2,1)...) fusion(bf16[16,3,128,3,128]{4,3,2,1,0:T(4,128)(2,1)} %reshape.333), kind=kLoop, calls=%fused_computation.73 | loop fusion | bytes 9437184 | tf_op jit(solution)/shard_map/slice | solution.py:65
  108.0 3.5 %copy.69 = bf16[16,1,128,1,128]{2,4,0,3,1:T(8,128)(2,1)} copy(bf16[16,1,128,1,128]{4,3,2,1,0:T(2,128)(2,1)} %get-tuple-element.13) | data formatting | bytes 1048576
  111.4 3.5 %copy.71 = bf16[16,1,128,1,128]{2,4,0,3,1:T(8,128)(2,1)} copy(bf16[16,1,128,1,128]{4,3,2,1,0:T(2,128)(2,1)} %get-tuple-element.12) | data formatting | bytes 1048576
  114.9 2.1 fusion.11
  117.1 2.3 fusion.35
  119.4 3.5 %copy.72 = bf16[16,1,128,1,128]{2,4,0,3,1:T(8,128)(2,1)} copy(bf16[16,1,128,1,128]{4,3,2,1,0:T(2,128)(2,1)} %get-tuple-element.11) | data formatting | bytes 1048576
  122.8 3.5 %copy.74 = bf16[16,1,128,1,128]{2,4,0,3,1:T(8,128)(2,1)} copy(bf16[16,1,128,1,128]{4,3,2,1,0:T(2,128)(2,1)} %get-tuple-element.10) | data formatting | bytes 1048576
  126.3 2.3 fusion.32
  128.6 3.5 %copy.75 = bf16[16,1,128,1,128]{2,4,0,3,1:T(8,128)(2,1)} copy(bf16[16,1,128,1,128]{4,3,2,1,0:T(2,128)(2,1)} %get-tuple-element.9) | data formatting | bytes 1048576
  132.1 3.5 %copy.76 = bf16[16,1,128,1,128]{2,4,0,3,1:T(8,128)(2,1)} copy(bf16[16,1,128,1,128]{4,3,2,1,0:T(2,128)(2,1)} %get-tuple-element.8) | data formatting | bytes 1048576
  135.6 1.8 copy.78
  137.4 2.3 fusion.28
  139.7 1.8 copy.79
  142.3 1.7 convolution_add_fusion.2
  148.4 6.1 %copy.59 = bf16[16,1,128,5,128]{4,3,2,0,1:T(8,128)(2,1)} copy(bf16[16,1,128,5,128]{2,4,0,3,1:T(8,128)(2,1)} %fusion.13) | data formatting | bytes 5242880 | tf_op jit(solution)/shard_map/stack | solution.py:70
  154.4 4.5 %convert_element_type.33 = bf16[16,81920]{1,0:T(8,128)(2,1)S(1)} reshape(bf16[16,1,128,5,128]{4,3,2,0,1:T(8,128)(2,1)} %copy.59) | data formatting | bytes 5242880 | tf_op jit(solution)/shard_map/convert_element_type | solution.py:70
  158.9 4.5 %stack.51 = bf16[4,16,81920]{2,1,0:T(8,128)(2,1)} broadcast(bf16[16,81920]{1,0:T(8,128)(2,1)S(1)} %convert_element_type.33), dimensions={1,2} | broadcast | bytes 13107200 | tf_op jit(solution)/shard_map/stack | solution.py:88
  163.4 8.0 %all-to-all-start = ((bf16[4,16,81920]{2,1,0:T(8,128)(2,1)}), bf16[4,16,81920]{2,1,0:T(8,128)(2,1)}, u32[]{:S(2)}, u32[]{:S(2)}) async-start(bf16[4,16,81920]{2,1,0:T(8,128)(2,1)} %stack.51), calls=%async_computation | async-start | bytes 20971520 | tf_op jit(solution)/shard_map/all_to_all | solution.py:88
  171.4 7.2 %collective-permute-start.1 = (bf16[128,384]{1,0:T(8,128)(2,1)S(1)}, bf16[128,384]{1,0:T(8,128)(2,1)S(1)}, u32[]{:S(2)}, u32[]{:S(2)}) collective-permute-start(bf16[128,384]{1,0:T(8,128)(2,1)S(1)} %copy-done.6), channel_id=1, source_target_pairs={{4,0},{8,4},{12,8},{16,12},{20,16},{24,20},{28,24},{32,28},{36,32}... | collective-permute-start | bytes 294920 | tf_op jit(solution)/shard_map/ppermute | solution.py:18
  178.6 1.6 copy.34
  180.2 1.9 copy.35
  182.3 106.1 %collective-permute-done = bf16[128,384]{1,0:T(8,128)(2,1)S(1)} collective-permute-done((bf16[128,384]{1,0:T(8,128)(2,1)S(1)}, bf16[128,384]{1,0:T(8,128)(2,1)S(1)}, u32[]{:S(2)}, u32[]{:S(2)}) %collective-permute-start) | collective-permute-done | bytes 98336 | tf_op jit(solution)/shard_map/ppermute | solution.py:16
  297.7 6.1 %copy.44 = bf16[16,1,128,5,128]{4,3,2,0,1:T(8,128)(2,1)} copy(bf16[16,1,128,5,128]{2,4,0,3,1:T(8,128)(2,1)} %fusion.9) | data formatting | bytes 5242880 | tf_op jit(solution)/shard_map/stack | solution.py:52
  303.8 4.5 %convert_element_type.32 = bf16[16,81920]{1,0:T(8,128)(2,1)S(1)} reshape(bf16[16,1,128,5,128]{4,3,2,0,1:T(8,128)(2,1)} %copy.44) | data formatting | bytes 5242880 | tf_op jit(solution)/shard_map/convert_element_type | solution.py:52
  308.3 5.5 %fusion.52 = f32[16,64]{1,0:T(8,128)S(1)} fusion(bf16[16,81920]{1,0:T(8,128)(2,1)S(1)} %convert_element_type.32, bf16[64,81920]{1,0:T(8,128)(2,1)} %bitcast.71), kind=kOutput, calls=%fused_computation.75 | convolution fusion | flops 167772160 | bytes 13111296 | tf_op jit(solution)/shard_map/pl,ql->pq/dot_general | solution.py:84
  314.0 15.8 %all_to_all.10 = f32[32,1,1024]{2,1,0:T(1,128)S(1)} all-to-all(f32[32,1,1024]{2,1,0:T(1,128)S(1)} %reshape.360), channel_id=1, replica_groups=mesh['ao'=32,'aux'=4] {'ao'}, dimensions={0} | all-to-all | bytes 262144 | tf_op jit(solution)/shard_map/all_to_all | solution.py:27
  (58 shorter events, 19.4 us)
Async XLA Ops:
  0.0 11.7 %copy-start.7 = (bf16[128,384]{1,0:T(8,128)(2,1)S(1)}, bf16[128,384]{1,0:T(8,128)(2,1)}, u32[]{:S(2)}) copy-start(bf16[128,384]{1,0:T(8,128)(2,1)} %param.7) | copy-start | bytes 294916
  2.5 71.3 %collective-permute-start.2 = (bf16[16,128,384]{2,1,0:T(8,128)(2,1)S(1)}, bf16[16,128,384]{2,1,0:T(8,128)(2,1)S(1)}, u32[]{:S(2)}, u32[]{:S(2)}) collective-permute-start(bf16[16,128,384]{2,1,0:T(8,128)(2,1)S(1)} %broadcast_multiply_fusion), channel_id=1, source_target_pairs={{0,4},{4,8},{8,12},{12,16},{16,20},{20,24},{24,28},{28,32},{32,36}... | collective-permute-start | bytes 4718600 | tf_op jit(solution)/shard_map/ppermute | solution.py:16
  7.0 70.3 %collective-permute-start.3 = (bf16[16,128,384]{2,1,0:T(8,128)(2,1)S(1)}, bf16[16,128,384]{2,1,0:T(8,128)(2,1)}, u32[]{:S(2)}, u32[]{:S(2)}) collective-permute-start(bf16[16,128,384]{2,1,0:T(8,128)(2,1)S(1)} %broadcast_multiply_fusion), channel_id=1, source_target_pairs={{4,0},{8,4},{12,8},{16,12},{20,16},{24,20},{28,24},{32,28},{36,32}... | collective-permute-start | bytes 4718600 | tf_op jit(solution)/shard_map/ppermute | solution.py:18
  139.7 4.2 %copy-start.1 = (f32[16,128,128]{2,1,0:T(8,128)S(1)}, f32[16,128,128]{2,1,0:T(8,128)}, u32[]{:S(2)}) copy-start(f32[16,128,128]{2,1,0:T(8,128)} %fusion.35) | copy-start | bytes 3145732
  141.5 2.5 copy-start.3
  142.2 2.8 copy-start.4
  144.0 2.2 copy-start.2
  144.0 2.2 copy-start.5
  163.4 8.0 %copy-start.6 = (bf16[128,384]{1,0:T(8,128)(2,1)S(1)}, bf16[128,384]{1,0:T(8,128)(2,1)}, u32[]{:S(2)}) copy-start(bf16[128,384]{1,0:T(8,128)(2,1)} %param.6) | copy-start | bytes 294916
  163.4 15.2 %copy-start = (bf16[16,128,384]{2,1,0:T(8,128)(2,1)S(1)}, bf16[16,128,384]{2,1,0:T(8,128)(2,1)}, u32[]{:S(2)}) copy-start(bf16[16,128,384]{2,1,0:T(8,128)(2,1)} %param.4) | copy-start | bytes 4718596
  163.4 144.9 %all-to-all-start = ((bf16[4,16,81920]{2,1,0:T(8,128)(2,1)}), bf16[4,16,81920]{2,1,0:T(8,128)(2,1)}, u32[]{:S(2)}, u32[]{:S(2)}) async-start(bf16[4,16,81920]{2,1,0:T(8,128)(2,1)} %stack.51), calls=%async_computation | async-start | bytes 20971520 | tf_op jit(solution)/shard_map/all_to_all | solution.py:88
  171.4 117.1 %collective-permute-start = (bf16[128,384]{1,0:T(8,128)(2,1)S(1)}, bf16[128,384]{1,0:T(8,128)(2,1)S(1)}, u32[]{:S(2)}, u32[]{:S(2)}) collective-permute-start(bf16[128,384]{1,0:T(8,128)(2,1)S(1)} %copy-done.6), channel_id=1, source_target_pairs={{0,4},{4,8},{8,12},{12,16},{16,20},{20,24},{24,28},{28,32},{32,36}... | collective-permute-start | bytes 294920 | tf_op jit(solution)/shard_map/ppermute | solution.py:16
  171.4 117.6 %collective-permute-start.1 = (bf16[128,384]{1,0:T(8,128)(2,1)S(1)}, bf16[128,384]{1,0:T(8,128)(2,1)S(1)}, u32[]{:S(2)}, u32[]{:S(2)}) collective-permute-start(bf16[128,384]{1,0:T(8,128)(2,1)S(1)} %copy-done.6), channel_id=1, source_target_pairs={{4,0},{8,4},{12,8},{16,12},{20,16},{24,20},{28,24},{32,28},{36,32}... | collective-permute-start | bytes 294920 | tf_op jit(solution)/shard_map/ppermute | solution.py:18
